TPU v7x, 256 devices: a whole 4x4x8 slice. The times are simulated.
256 devices in a mesh: chain: 8 (over y, core), cols: 32 (over x, z).
Axes of the slice: x: 4, y: 4, z: 8, core: 2. Of those that a mesh axis runs over, the one named last changes fastest.
Arguments:
- factor: float32 [4608, 4608], P(('chain', 'cols')), may hold values from -2 to 2, as said below
- right_side: float32 [4608, 16384], P('chain', 'cols'), may hold values from -6 to 6
- occ_order: int32 [64], replicated, may hold values from 0 to 63, each once
- cabs_order: int32 [256], replicated, may hold values from 0 to 255, each once
Outputs:
- fitted: float32 [64, 256, 4608], P('cols', None, 'chain')
Inputs may be any that keep to these rules, and one draw needn't show every extreme that they name: factor is lower triangular: zero above the diagonal, its diagonal between 1 and 2.
All inputs are finite; a program needn't handle non-finite values.
Results may differ from a plain program's by a relative error of at most 0.00017.
Values sent between devices are 32-bit elements; how exact they have to be, the bound alone decides.
No kernel may reach another device: no remote copies, remote signals or barrier semaphores. Data moves between devices by JAX's collectives and lax.ppermute only.
A program may use at most 128 MiB of HBM per device.

v0:
```python
import jax
import jax.numpy as jnp
from jax import lax
from jax.sharding import PartitionSpec as P


def from_root(value, axis, root):
    return lax.dynamic_index_in_dim(lax.all_gather(value, axis), root, 0, keepdims=False)


def product(left, right):
    return jnp.dot(left, right, precision=lax.Precision.HIGHEST, preferred_element_type=jnp.float32)


def per_device(factor, right_side, occ_order, cabs_order):
    chain_size = lax.axis_size("chain")
    position = lax.axis_index("chain")
    factor_row = lax.all_gather(factor, "cols", axis=0, tiled=True)
    aux_rows = factor_row.shape[0]
    diag_block = lax.dynamic_slice_in_dim(factor_row, position * aux_rows, aux_rows, 1)
    identity = jnp.eye(aux_rows, dtype=jnp.float32)
    inverse = jax.scipy.linalg.solve_triangular(diag_block, identity, lower=True)

    def settle(residual):
        return product(inverse, residual)

    def blank(residual):
        return jnp.zeros_like(residual)

    residual = right_side
    solution = jnp.zeros_like(right_side)
    for section in range(chain_size):
        solved = lax.cond(position == section, settle, blank, residual)
        solution = solution + solved
        if section + 1 < chain_size:
            arrived = from_root(solved, "chain", section)
            coupling = factor_row[:, section * aux_rows : (section + 1) * aux_rows]

            def lower_block(current, arrived=arrived, coupling=coupling):
                return current - product(coupling, arrived)

            def keep_block(current):
                return current

            residual = lax.cond(position > section, lower_block, keep_block, residual)
    occ_total = occ_order.shape[0]
    cabs_local = right_side.shape[1] // occ_total
    cols_size = lax.axis_size("cols")
    occ_local = occ_total // cols_size
    grid = solution.reshape(aux_rows, cabs_local, occ_total)
    grid = jnp.take(grid, occ_order, axis=2)
    grid = grid.reshape(aux_rows, cabs_local, cols_size, occ_local)
    grid = jnp.transpose(grid, (2, 3, 1, 0))
    moved = jnp.take(
        lax.all_to_all(grid, "cols", split_axis=0, concat_axis=2, tiled=True), cabs_order, axis=2
    )
    return moved.reshape(occ_local, moved.shape[2], aux_rows)


def solution(mesh):
    in_specs = (P(("chain", "cols"), None), P("chain", "cols"), P(), P())
    out_specs = P("cols", None, "chain")
    return jax.shard_map(
        per_device, mesh=mesh, in_specs=in_specs, out_specs=out_specs, check_vma=False
    )
```

profile of v0, /device:TPU:33, one launch (start us, length us, event | category | flops | bytes accessed | tf_op | source)
XLA Modules:
  0.0 740.3 jit_solution(2091140109980776723)
XLA Ops:
  9.3 128.3 %all-gather.31.cloned.1.call-done = f32[32,18,4608]{2,1,0:T(8,128)} async-done(((f32[1,18,4608]{2,1,0:T(8,128)}), f32[32,18,4608]{2,1,0:T(8,128)}) %all-gather.31.cloned.1.call-update) | async-done | bytes 10616848 | tf_op jit(solution)/shard_map/all_gather | solution.py:18
  137.6 11.4 %reshape.89 = f32[576,4608]{1,0:T(8,128)} reshape(f32[32,18,4608]{2,1,0:T(8,128)} %all-gather.31.cloned.1.call-done) | data formatting | bytes 21233664
  150.7 10.5 %while.1 = (s32[]{:T(128)}, f32[576,576]{1,0:T(8,128)S(1)}, s32[4,2]{0,1:T(2,128)S(1)}, f32[4,128,128]{2,1,0:T(8,128)}, s32[]{:T(128)}) while((s32[]{:T(128)}, f32[576,576]{1,0:T(8,128)S(1)}, s32[4,2]{0,1:T(2,128)S(1)}, f32[4,128,128]{2,1,0:T(8,128)}, s32[]{:T(128)}) %tuple.169), condition=%wide.while_cond, body=%wide.while_body.sunk | while | flops 2 | bytes 132705 | solution.py:22
  151.4 2.0 bitcast_dynamic-update-slice_fusion.2
  154.0 2.0 bitcast_dynamic-update-slice_fusion.2
  156.7 2.0 bitcast_dynamic-update-slice_fusion.2
  162.6 49.8 %custom-call.4 = f32[5,128,128]{1,2,0:T(8,128)} custom-call(f32[5,128,128]{2,1,0:T(8,128)S(1)} %pad_maximum_fusion), custom_call_target="InvertDiagBlocksLowerTriangular" | custom-call | tf_op jit(solution)/shard_map/jit(_solve_triangular)/triangular_solve | solution.py:22
  220.5 2.0 fusion.57
  224.1 56.9 %all-gather.17.cloned.1.call-done = f32[4608,512]{1,0:T(8,128)} async-done(((f32[576,512]{1,0:T(8,128)}), f32[4608,512]{1,0:T(8,128)}) %all-gather.17.cloned.1.call-update) | async-done | bytes 9437200 | tf_op jit(solution)/shard_map/all_gather | solution.py:8
  281.0 5.0 conditional.16
  281.2 4.8 fusion.2
  286.0 4.1 conditional.17
  286.0 4.1 fusion.84
  290.2 55.5 %all-gather.19.cloned.1.call-done = f32[4608,512]{1,0:T(8,128)} async-done(((f32[576,512]{1,0:T(8,128)}), f32[4608,512]{1,0:T(8,128)}) %all-gather.19.cloned.1.call-update) | async-done | bytes 9437200 | tf_op jit(solution)/shard_map/all_gather | solution.py:8
  347.0 63.7 %all-gather.21.cloned.1.call-done = f32[4608,512]{1,0:T(8,128)} async-done(((f32[576,512]{1,0:T(8,128)}), f32[4608,512]{1,0:T(8,128)}) %all-gather.21.cloned.1.call-update) | async-done | bytes 9437200 | tf_op jit(solution)/shard_map/all_gather | solution.py:8
  412.4 63.4 %all-gather.23.cloned.1.call-done = f32[4608,512]{1,0:T(8,128)} async-done(((f32[576,512]{1,0:T(8,128)}), f32[4608,512]{1,0:T(8,128)}) %all-gather.23.cloned.1.call-update) | async-done | bytes 9437200 | tf_op jit(solution)/shard_map/all_gather | solution.py:8
  477.1 64.9 %all-gather.25.cloned.1.call-done = f32[4608,512]{1,0:T(8,128)} async-done(((f32[576,512]{1,0:T(8,128)}), f32[4608,512]{1,0:T(8,128)}) %all-gather.25.cloned.1.call-update) | async-done | bytes 9437200 | tf_op jit(solution)/shard_map/all_gather | solution.py:8
  543.4 64.6 %all-gather.27.cloned.1.call-done = f32[4608,512]{1,0:T(8,128)} async-done(((f32[576,512]{1,0:T(8,128)}), f32[4608,512]{1,0:T(8,128)}) %all-gather.27.cloned.1.call-update) | async-done | bytes 9437200 | tf_op jit(solution)/shard_map/all_gather | solution.py:8
  609.4 63.8 %all-gather.29.cloned.1.call-done = f32[4608,512]{1,0:T(8,128)} async-done(((f32[576,512]{1,0:T(8,128)}), f32[4608,512]{1,0:T(8,128)}) %all-gather.29.cloned.1.call-update) | async-done | bytes 9437200 | tf_op jit(solution)/shard_map/all_gather | solution.py:8
  674.6 4.9 add_add_fusion
  682.6 9.9 %all-to-all-start = ((f32[32,2,8,576]{3,2,1,0:T(8,128)}), f32[32,2,8,576]{3,2,1,0:T(8,128)S(1)}, u32[]{:S(2)}, u32[]{:S(2)}) async-start(f32[32,2,8,576]{3,2,1,0:T(8,128)} %select_bitcast_fusion.1), calls=%async_computation | async-start | bytes 2621440 | tf_op jit(solution)/shard_map/all_to_all | solution.py:55
  692.5 34.0 %all-to-all-done = f32[32,2,8,576]{3,2,1,0:T(8,128)S(1)} async-done(((f32[32,2,8,576]{3,2,1,0:T(8,128)}), f32[32,2,8,576]{3,2,1,0:T(8,128)S(1)}, u32[]{:S(2)}, u32[]{:S(2)}) %all-to-all-start) | async-done | bytes 1179680 | tf_op jit(solution)/shard_map/all_to_all | solution.py:55
  727.5 2.2 gather_fusion.1
  730.8 2.2 copy.71
  (88 shorter events, 41.9 us)
Async XLA Ops:
  6.5 131.1 %all-gather.31.cloned.1.call-start = ((), (), s32[]{:S(2)}) async-start(), calls=%async_computation.8 | async-start | bytes 14598144 | tf_op jit(solution)/shard_map/all_gather | solution.py:18
  7.8 273.2 %all-gather.17.cloned.1.call-start = ((), (), s32[]{:S(2)}) async-start(), calls=%async_computation.1 | async-start | bytes 10616832 | tf_op jit(solution)/shard_map/all_gather | solution.py:8
  161.3 1.3 copy-start.1
  212.3 4.0 copy-start
  215.0 2.9 copy-start.2
  224.1 121.7 %all-gather.19.cloned.1.call-start = ((), (), s32[]{:S(2)}) async-start(), calls=%async_computation.2 | async-start | bytes 10616832 | tf_op jit(solution)/shard_map/all_gather | solution.py:8
  290.1 120.5 %all-gather.21.cloned.1.call-start = ((), (), s32[]{:S(2)}) async-start(), calls=%async_computation.3 | async-start | bytes 10616832 | tf_op jit(solution)/shard_map/all_gather | solution.py:8
  347.0 128.8 %all-gather.23.cloned.1.call-start = ((), (), s32[]{:S(2)}) async-start(), calls=%async_computation.4 | async-start | bytes 10616832 | tf_op jit(solution)/shard_map/all_gather | solution.py:8
  412.4 129.6 %all-gather.25.cloned.1.call-start = ((), (), s32[]{:S(2)}) async-start(), calls=%async_computation.5 | async-start | bytes 10616832 | tf_op jit(solution)/shard_map/all_gather | solution.py:8
  477.0 131.0 %all-gather.27.cloned.1.call-start = ((), (), s32[]{:S(2)}) async-start(), calls=%async_computation.6 | async-start | bytes 10616832 | tf_op jit(solution)/shard_map/all_gather | solution.py:8
  543.3 129.9 %all-gather.29.cloned.1.call-start = ((), (), s32[]{:S(2)}) async-start(), calls=%async_computation.7 | async-start | bytes 10616832 | tf_op jit(solution)/shard_map/all_gather | solution.py:8
  608.0 1.2 copy-start.4
  608.0 1.3 copy-start.3
  682.6 43.8 %all-to-all-start = ((f32[32,2,8,576]{3,2,1,0:T(8,128)}), f32[32,2,8,576]{3,2,1,0:T(8,128)S(1)}, u32[]{:S(2)}, u32[]{:S(2)}) async-start(f32[32,2,8,576]{3,2,1,0:T(8,128)} %select_bitcast_fusion.1), calls=%async_computation | async-start | bytes 2621440 | tf_op jit(solution)/shard_map/all_to_all | solution.py:55
Sparse Core Ops, SparseCore 0:
  9.9 127.6 all-gather.30
  224.2 56.7 all-gather.16
  290.3 55.4 all-gather.18
  347.4 63.2 all-gather.20
  412.5 63.2 all-gather.22
  477.5 64.4 all-gather.24
  543.8 64.1 all-gather.26
  609.9 63.3 all-gather.28
where the time goes:
time: 749 us; the launch traced here: 740 us
  waiting for transfers between devices  595 us (79%)
  other arithmetic  61.4 us (8%)
  local copies, waits for them, and re-layouts  38.8 us (5%)
  matrix products  19.3 us (3%)
  between operations  14.3 us (2%)
  starting transfers between devices  10.1 us (1%)
    all_gather x7, waiting for transfers between devices, from_root(): lax.all_gather(value, axis)  433 us
    all_gather x1, waiting for transfers between devices, per_device(): factor_row = lax.all_gather(factor, 'cols', axis=0, tiled=True)  128 us
    another operation x7, other arithmetic, per_device(): jax.scipy.linalg.solve_triangular(diag_block, identity, lower=True)  52.8 us
    all_to_all x1, waiting for transfers between devices, per_device(): lax.all_to_all(grid, 'cols', split_axis=0, concat_axis=2, tiled=True)  34 us
    another operation x19, local copies, waits for them, and re-layouts  18.8 us
  transfers between devices with their start and end apart: 9, of which 9 were waited for; matrix products, arithmetic and copies ran while one was open for 0% of the time, Pallas kernels for 0%

commit v1 on v0

--- a/solution.py
+++ b/solution.py
@@ -2,6 +2,18 @@
 import jax.numpy as jnp
 from jax import lax
 from jax.sharding import PartitionSpec as P
+
+
+def collect(value, axis, dim):
+    ways, here = (lax.axis_size(axis), lax.axis_index(axis))
+    grown, reach = (value, 1)
+    while reach < ways:
+        theirs = lax.ppermute(grown, axis, [(d, d ^ reach) for d in range(ways)])
+        mine_first = jnp.concatenate([grown, theirs], axis=dim)
+        theirs_first = jnp.concatenate([theirs, grown], axis=dim)
+        grown = jnp.where(here & reach == 0, mine_first, theirs_first)
+        reach = 2 * reach
+    return grown
 
 
 def from_root(value, axis, root):
@@ -15,7 +27,7 @@
 def per_device(factor, right_side, occ_order, cabs_order):
     chain_size = lax.axis_size("chain")
     position = lax.axis_index("chain")
-    factor_row = lax.all_gather(factor, "cols", axis=0, tiled=True)
+    factor_row = collect(factor, "cols", 0)
     aux_rows = factor_row.shape[0]
     diag_block = lax.dynamic_slice_in_dim(factor_row, position * aux_rows, aux_rows, 1)
     identity = jnp.eye(aux_rows, dtype=jnp.float32)

time: 749 us -> 913 us (1.22)
  waiting for transfers between devices: 595 us -> 741 us
  other arithmetic: 61.4 us -> 80.3 us
  starting transfers between devices: 10.1 us -> 21.2 us
    ppermute x0 -> x5, waiting for transfers between devices: none -> 246 us  [collect(): theirs = lax.ppermute(grown, axis, [(d, d ^ reach) for d in range(ways)])]
    all_gather x1 -> x0, waiting for transfers between devices: 128 us -> none  [per_device(): factor_row = lax.all_gather(factor, 'cols', axis=0, tiled=True)]
    all_gather x7, waiting for transfers between devices: 433 us -> 461 us  [from_root(): lax.all_gather(value, axis)]
    select_n x0 -> x5, other arithmetic: none -> 20.3 us  [collect(): grown = jnp.where(here & reach == 0, mine_first, theirs_first)]
    ppermute x0 -> x5, starting transfers between devices: none -> 11.2 us  [collect(): theirs = lax.ppermute(grown, axis, [(d, d ^ reach) for d in range(ways)])]
  transfers between devices with their start and end apart: 9 -> 13, of which waited for: 9 -> 13; matrix products, arithmetic and copies ran while one was open for 0% -> 0% of each run, Pallas kernels for 0% -> 0%
where the time goes in v1:
time: 913 us; the launch traced here: 909 us
  waiting for transfers between devices  741 us (81%)
  other arithmetic  80.3 us (9%)
  local copies, waits for them, and re-layouts  31.4 us (3%)
  starting transfers between devices  21.2 us (2%)
  matrix products  19.3 us (2%)
  between operations  14.1 us (2%)
    all_gather x7, waiting for transfers between devices, from_root(): lax.all_gather(value, axis)  461 us
    ppermute x5, waiting for transfers between devices, collect(): theirs = lax.ppermute(grown, axis, [(d, d ^ reach) for d in range(ways)])  246 us
    another operation x7, other arithmetic, per_device(): jax.scipy.linalg.solve_triangular(diag_block, identity, lower=True)  51.3 us
    all_to_all x1, waiting for transfers between devices, per_device(): lax.all_to_all(grid, 'cols', split_axis=0, concat_axis=2, tiled=True)  34 us
    select_n x5, other arithmetic, collect(): grown = jnp.where(here & reach == 0, mine_first, theirs_first)  20.3 us
    another operation x19, local copies, waits for them, and re-layouts  18.6 us
  transfers between devices with their start and end apart: 13, of which 13 were waited for; matrix products, arithmetic and copies ran while one was open for 0% of the time, Pallas kernels for 0%

profile of v1, /device:TPU:33, one launch (start us, length us, event | category | flops | bytes accessed | tf_op | source)
XLA Modules:
  0.0 908.9 jit_solution(4625729488481041979)
XLA Ops:
  7.9 11.0 %collective-permute-done = f32[18,4608]{1,0:T(8,128)S(1)} collective-permute-done((f32[18,4608]{1,0:T(8,128)S(1)}, f32[18,4608]{1,0:T(8,128)S(1)}, u32[]{:S(2)}, u32[]{:S(2)}) %collective-permute-start) | collective-permute-done | bytes 331808 | tf_op jit(solution)/shard_map/ppermute | solution.py:11
  22.1 31.9 %collective-permute-done.1 = f32[36,4608]{1,0:T(8,128)} collective-permute-done((f32[36,4608]{1,0:T(8,128)S(1)}, f32[36,4608]{1,0:T(8,128)}, u32[]{:S(2)}, u32[]{:S(2)}) %collective-permute-start.1) | collective-permute-done | bytes 663584 | tf_op jit(solution)/shard_map/ppermute | solution.py:11
  59.5 35.7 %collective-permute-done.2 = f32[72,4608]{1,0:T(8,128)} collective-permute-done((f32[72,4608]{1,0:T(8,128)S(1)}, f32[72,4608]{1,0:T(8,128)}, u32[]{:S(2)}, u32[]{:S(2)}) %collective-permute-start.2) | collective-permute-done | bytes 1327136 | tf_op jit(solution)/shard_map/ppermute | solution.py:11
  99.9 56.7 %collective-permute-done.3 = f32[144,4608]{1,0:T(8,128)} collective-permute-done((f32[144,4608]{1,0:T(8,128)}, f32[144,4608]{1,0:T(8,128)}, u32[]{:S(2)}, u32[]{:S(2)}) %collective-permute-start.3) | collective-permute-done | bytes 2654240 | tf_op jit(solution)/shard_map/ppermute | solution.py:11
  156.6 6.4 maximum_select_fusion.1
  167.4 111.2 %collective-permute-done.4 = f32[288,4608]{1,0:T(8,128)} collective-permute-done((f32[288,4608]{1,0:T(8,128)}, f32[288,4608]{1,0:T(8,128)}, u32[]{:S(2)}, u32[]{:S(2)}) %collective-permute-start.4) | collective-permute-done | bytes 5308448 | tf_op jit(solution)/shard_map/ppermute | solution.py:11
  278.6 8.7 maximum_select_fusion
  287.3 4.0 copy-done
  291.7 10.4 %while.1 = (s32[]{:T(128)}, f32[576,576]{1,0:T(8,128)S(1)}, s32[4,2]{0,1:T(2,128)S(1)}, f32[4,128,128]{2,1,0:T(8,128)}, s32[]{:T(128)}) while((s32[]{:T(128)}, f32[576,576]{1,0:T(8,128)S(1)}, s32[4,2]{0,1:T(2,128)S(1)}, f32[4,128,128]{2,1,0:T(8,128)}, s32[]{:T(128)}) %tuple.161), condition=%wide.while_cond, body=%wide.while_body.sunk | while | flops 2 | bytes 132705 | solution.py:34
  303.3 49.8 %custom-call.4 = f32[5,128,128]{1,2,0:T(8,128)} custom-call(f32[5,128,128]{2,1,0:T(8,128)S(1)} %pad_maximum_fusion), custom_call_target="InvertDiagBlocksLowerTriangular" | custom-call | tf_op jit(solution)/shard_map/jit(_solve_triangular)/triangular_solve | solution.py:34
  364.9 84.8 %all-gather.15.cloned.1.call-done = f32[4608,512]{1,0:T(8,128)} async-done(((f32[576,512]{1,0:T(8,128)}), f32[4608,512]{1,0:T(8,128)}) %all-gather.15.cloned.1.call-update) | async-done | bytes 9437200 | tf_op jit(solution)/shard_map/all_gather | solution.py:20
  449.6 5.3 conditional.16
  450.1 4.8 fusion.2
  454.9 4.1 conditional.17
  455.0 4.1 fusion.84
  459.1 55.5 %all-gather.17.cloned.1.call-done = f32[4608,512]{1,0:T(8,128)} async-done(((f32[576,512]{1,0:T(8,128)}), f32[4608,512]{1,0:T(8,128)}) %all-gather.17.cloned.1.call-update) | async-done | bytes 9437200 | tf_op jit(solution)/shard_map/all_gather | solution.py:20
  515.9 63.7 %all-gather.19.cloned.1.call-done = f32[4608,512]{1,0:T(8,128)} async-done(((f32[576,512]{1,0:T(8,128)}), f32[4608,512]{1,0:T(8,128)}) %all-gather.19.cloned.1.call-update) | async-done | bytes 9437200 | tf_op jit(solution)/shard_map/all_gather | solution.py:20
  581.0 63.4 %all-gather.21.cloned.1.call-done = f32[4608,512]{1,0:T(8,128)} async-done(((f32[576,512]{1,0:T(8,128)}), f32[4608,512]{1,0:T(8,128)}) %all-gather.21.cloned.1.call-update) | async-done | bytes 9437200 | tf_op jit(solution)/shard_map/all_gather | solution.py:20
  645.8 64.9 %all-gather.23.cloned.1.call-done = f32[4608,512]{1,0:T(8,128)} async-done(((f32[576,512]{1,0:T(8,128)}), f32[4608,512]{1,0:T(8,128)}) %all-gather.23.cloned.1.call-update) | async-done | bytes 9437200 | tf_op jit(solution)/shard_map/all_gather | solution.py:20
  712.1 64.6 %all-gather.25.cloned.1.call-done = f32[4608,512]{1,0:T(8,128)} async-done(((f32[576,512]{1,0:T(8,128)}), f32[4608,512]{1,0:T(8,128)}) %all-gather.25.cloned.1.call-update) | async-done | bytes 9437200 | tf_op jit(solution)/shard_map/all_gather | solution.py:20
  778.2 63.8 %all-gather.27.cloned.1.call-done = f32[4608,512]{1,0:T(8,128)} async-done(((f32[576,512]{1,0:T(8,128)}), f32[4608,512]{1,0:T(8,128)}) %all-gather.27.cloned.1.call-update) | async-done | bytes 9437200 | tf_op jit(solution)/shard_map/all_gather | solution.py:20
  843.6 4.9 add_add_fusion
  851.5 9.8 %all-to-all-start = ((f32[32,2,8,576]{3,2,1,0:T(8,128)}), f32[32,2,8,576]{3,2,1,0:T(8,128)S(1)}, u32[]{:S(2)}, u32[]{:S(2)}) async-start(f32[32,2,8,576]{3,2,1,0:T(8,128)} %select_bitcast_fusion.1), calls=%async_computation | async-start | bytes 2621440 | tf_op jit(solution)/shard_map/all_to_all | solution.py:67
  861.3 34.0 %all-to-all-done = f32[32,2,8,576]{3,2,1,0:T(8,128)S(1)} async-done(((f32[32,2,8,576]{3,2,1,0:T(8,128)}), f32[32,2,8,576]{3,2,1,0:T(8,128)S(1)}, u32[]{:S(2)}, u32[]{:S(2)}) %all-to-all-start) | async-done | bytes 1179680 | tf_op jit(solution)/shard_map/all_to_all | solution.py:67
  (103 shorter events, 69.0 us)
Async XLA Ops:
  6.5 1.4 copy-start.3
  6.5 443.1 %all-gather.15.cloned.1.call-start = ((), (), s32[]{:S(2)}) async-start(), calls=%async_computation.1 | async-start | bytes 10616832 | tf_op jit(solution)/shard_map/all_gather | solution.py:20
  7.9 11.0 %collective-permute-start = (f32[18,4608]{1,0:T(8,128)S(1)}, f32[18,4608]{1,0:T(8,128)S(1)}, u32[]{:S(2)}, u32[]{:S(2)}) collective-permute-start(f32[18,4608]{1,0:T(8,128)S(1)} %copy-done.3), channel_id=1, source_target_pairs={{0,1},{1,0},{2,3},{3,2},{4,5},{5,4},{6,7},{7,6},{8,9},{9,8},{10,11... | collective-permute-start | bytes 995336 | tf_op jit(solution)/shard_map/ppermute | solution.py:11
  19.1 35.0 %collective-permute-start.1 = (f32[36,4608]{1,0:T(8,128)S(1)}, f32[36,4608]{1,0:T(8,128)}, u32[]{:S(2)}, u32[]{:S(2)}) collective-permute-start(f32[36,4608]{1,0:T(8,128)S(1)} %maximum_select_fusion.4), channel_id=1, source_target_pairs={{0,2},{1,3},{2,0},{3,1},{4,6},{5,7},{6,4},{7,5},{8,10},{9,11},{10,... | collective-permute-start | bytes 1990664 | tf_op jit(solution)/shard_map/ppermute | solution.py:11
  55.6 39.5 %collective-permute-start.2 = (f32[72,4608]{1,0:T(8,128)S(1)}, f32[72,4608]{1,0:T(8,128)}, u32[]{:S(2)}, u32[]{:S(2)}) collective-permute-start(f32[72,4608]{1,0:T(8,128)S(1)} %maximum_select_fusion.3), channel_id=1, source_target_pairs={{0,4},{1,5},{2,6},{3,7},{4,0},{5,1},{6,2},{7,3},{8,12},{9,13},{10,... | collective-permute-start | bytes 3981320 | tf_op jit(solution)/shard_map/ppermute | solution.py:11
  98.7 57.9 %collective-permute-start.3 = (f32[144,4608]{1,0:T(8,128)}, f32[144,4608]{1,0:T(8,128)}, u32[]{:S(2)}, u32[]{:S(2)}) collective-permute-start(f32[144,4608]{1,0:T(8,128)} %maximum_select_fusion.2), channel_id=1, source_target_pairs={{0,8},{1,9},{2,10},{3,11},{4,12},{5,13},{6,14},{7,15},{8,0},{9,1},... | collective-permute-start | bytes 7962632 | tf_op jit(solution)/shard_map/ppermute | solution.py:11
  163.0 115.6 %collective-permute-start.4 = (f32[288,4608]{1,0:T(8,128)}, f32[288,4608]{1,0:T(8,128)}, u32[]{:S(2)}, u32[]{:S(2)}) collective-permute-start(f32[288,4608]{1,0:T(8,128)} %maximum_select_fusion.1), channel_id=1, source_target_pairs={{0,16},{1,17},{2,18},{3,19},{4,20},{5,21},{6,22},{7,23},{8,24},{9,... | collective-permute-start | bytes 15925256 | tf_op jit(solution)/shard_map/ppermute | solution.py:11
  287.3 4.1 copy-start
  302.0 1.3 copy-start.2
  353.1 4.0 copy-start.1
  355.7 2.9 copy-start.4
  364.8 149.8 %all-gather.17.cloned.1.call-start = ((), (), s32[]{:S(2)}) async-start(), calls=%async_computation.2 | async-start | bytes 10616832 | tf_op jit(solution)/shard_map/all_gather | solution.py:20
  459.1 120.5 %all-gather.19.cloned.1.call-start = ((), (), s32[]{:S(2)}) async-start(), calls=%async_computation.3 | async-start | bytes 10616832 | tf_op jit(solution)/shard_map/all_gather | solution.py:20
  515.9 128.5 %all-gather.21.cloned.1.call-start = ((), (), s32[]{:S(2)}) async-start(), calls=%async_computation.4 | async-start | bytes 10616832 | tf_op jit(solution)/shard_map/all_gather | solution.py:20
  581.0 129.7 %all-gather.23.cloned.1.call-start = ((), (), s32[]{:S(2)}) async-start(), calls=%async_computation.5 | async-start | bytes 10616832 | tf_op jit(solution)/shard_map/all_gather | solution.py:20
  645.7 131.1 %all-gather.25.cloned.1.call-start = ((), (), s32[]{:S(2)}) async-start(), calls=%async_computation.6 | async-start | bytes 10616832 | tf_op jit(solution)/shard_map/all_gather | solution.py:20
  712.1 129.9 %all-gather.27.cloned.1.call-start = ((), (), s32[]{:S(2)}) async-start(), calls=%async_computation.7 | async-start | bytes 10616832 | tf_op jit(solution)/shard_map/all_gather | solution.py:20
  776.8 1.2 copy-start.6
  776.8 1.3 copy-start.5
  851.5 43.8 %all-to-all-start = ((f32[32,2,8,576]{3,2,1,0:T(8,128)}), f32[32,2,8,576]{3,2,1,0:T(8,128)S(1)}, u32[]{:S(2)}, u32[]{:S(2)}) async-start(f32[32,2,8,576]{3,2,1,0:T(8,128)} %select_bitcast_fusion.1), calls=%async_computation | async-start | bytes 2621440 | tf_op jit(solution)/shard_map/all_to_all | solution.py:67
Sparse Core Ops, SparseCore 0:
  364.9 84.6 all-gather.14
  459.2 55.4 all-gather.16
  516.5 63.0 all-gather.18
  581.3 63.0 all-gather.20
  646.1 64.5 all-gather.22
  712.4 64.3 all-gather.24
  778.6 63.3 all-gather.26
